TPU v7x, 32 devices: a whole 2x2x4 slice. The times are simulated.
32 devices in a mesh: dp: 16 (over z, y, x), mp: 2 (over core).
Axes of the slice: x: 2, y: 2, z: 4, core: 2. Of those that a mesh axis runs over, the one named last changes fastest.
Arguments:
- tokens: bfloat16 [2, 512, 16, 768], P('mp', 'dp'), may hold values from -6 to 6
- cotangent: bfloat16 [2, 512, 16, 768], P('mp', 'dp'), may hold values from -6 to 6
- lengths: int32 [16], replicated, may hold values from 128 to 1024, as said below
- deal_order: int32 [16], replicated, may hold values from 0 to 15, as said below
- attn_in: bfloat16 [1, 3, 768, 768], P(None, None, 'dp', 'mp'), may hold values from -0.21875 to 0.21875
- attn_out: bfloat16 [1, 768, 768], P(None, 'mp', 'dp'), may hold values from -0.875 to 0.875
- ffn_in: bfloat16 [1, 768, 3072], P(None, 'dp', 'mp'), may hold values from -0.21875 to 0.21875
- ffn_out: bfloat16 [1, 3072, 768], P(None, 'mp', 'dp'), may hold values from -0.109375 to 0.109375
- attn_bias: bfloat16 [1, 2, 768], replicated, may hold values from -3 to 3
- ffn_bias: bfloat16 [1, 3072], replicated, may hold values from -3 to 3
- norm_gain: bfloat16 [1, 2, 768], replicated, may hold values from 0.5 to 1.5
- shifts: bfloat16 [1, 4, 768], replicated, may hold values from -3 to 3
Outputs:
- output: bfloat16 [2, 512, 16, 768], P('mp', 'dp')
- input_grad: bfloat16 [2, 512, 16, 768], P('mp', 'dp')
- attn_in_grad: float32 [1, 3, 768, 768], P(None, None, 'dp', 'mp')
- attn_out_grad: float32 [1, 768, 768], P(None, 'mp', 'dp')
- ffn_in_grad: float32 [1, 768, 3072], P(None, 'dp', 'mp')
- ffn_out_grad: float32 [1, 3072, 768], P(None, 'mp', 'dp')
- attn_bias_grad: float32 [1, 2, 768], replicated
- ffn_bias_grad: float32 [1, 3072], replicated
- norm_gain_grad: float32 [1, 2, 768], replicated
- shifts_grad: float32 [1, 4, 768], replicated
Inputs may be any that keep to these rules, and one draw needn't show every extreme that they name: `lengths`: some sequence has exactly 1024 valid tokens. `deal_order`: a permutation of the sequences; slot s is processed by data group s.
All inputs are finite; a program needn't handle non-finite values.
Results may differ from a plain program's by a relative error of at most 0.02.
Values may be sent and summed in bfloat16 or wider, within the bound.
No kernel may reach another device: no remote copies, remote signals or barrier semaphores. Data moves between devices by JAX's collectives and lax.ppermute only.
A program may use at most 128 MiB of HBM per device.

v0:
```python
import jax
import jax.numpy as jnp
from jax import lax
from jax.sharding import PartitionSpec as P

HEAD_DIM = 64


eps_norm = 1e-12
root_half = 0.7071067811865476
inv_root_two_pi = 0.3989422804014327
negative_fill = -1000000000.0


def gather_rows(rows_low):
    return lax.all_gather(rows_low, "mp", axis=0, tiled=True)


def gather_grads(rows_low):
    return lax.all_gather(rows_low, "mp", axis=0, tiled=True)


def spread_rows(make_term, row_count):
    return lax.psum_scatter(
        make_term(jnp.int32(0), row_count * lax.axis_size("mp")).astype(jnp.bfloat16),
        "mp",
        scatter_dimension=0,
        tiled=True,
    ).astype(jnp.float32)


def spread_grads(make_term, row_count):
    return lax.psum_scatter(
        make_term(jnp.int32(0), row_count * lax.axis_size("mp")).astype(jnp.bfloat16),
        "mp",
        scatter_dimension=0,
        tiled=True,
    ).astype(jnp.float32)


def fetch_weights(three_part, back_part, up_part, down_part):
    return (
        lax.all_gather(three_part, "dp", axis=1, tiled=True),
        lax.all_gather(back_part, "dp", axis=1, tiled=True),
        lax.all_gather(up_part, "dp", axis=0, tiled=True),
        lax.all_gather(down_part, "dp", axis=1, tiled=True),
    )


def fetch_again(three_part, back_part, up_part, down_part):
    return (
        lax.all_gather(three_part, "dp", axis=1, tiled=True),
        lax.all_gather(back_part, "dp", axis=1, tiled=True),
        lax.all_gather(up_part, "dp", axis=0, tiled=True),
        lax.all_gather(down_part, "dp", axis=1, tiled=True),
    )


def contract_rows(left_rows, right_rows):
    return lax.dot_general(
        left_rows, right_rows, (((0,), (0,)), ((), ())), preferred_element_type=jnp.float32
    )


def contract_cols(left_rows, right_rows):
    return lax.dot_general(
        left_rows, right_rows, (((1,), (1,)), ((), ())), preferred_element_type=jnp.float32
    )


def norm_forward(mixed_rows, gain, shift):
    center = mixed_rows - jnp.mean(mixed_rows, axis=1, keepdims=True)
    rstd_rows = lax.rsqrt(jnp.mean(center * center, axis=1, keepdims=True) + eps_norm)
    normed = center * rstd_rows
    return (normed * gain + shift, normed, rstd_rows)


def norm_backward(grad_rows, normed, rstd_rows, gain):
    scaled = grad_rows * gain
    inner = (
        scaled
        - jnp.mean(scaled, axis=1, keepdims=True)
        - normed * jnp.mean(scaled * normed, axis=1, keepdims=True)
    )
    return (rstd_rows * inner, jnp.sum(grad_rows * normed, axis=0), jnp.sum(grad_rows, axis=0))


def gelu_value(hidden_pre):
    return 0.5 * hidden_pre * (1.0 + lax.erf(hidden_pre * root_half))


def gelu_slope(hidden_pre):
    return (
        0.5 * (1.0 + lax.erf(hidden_pre * root_half))
        + hidden_pre * jnp.exp(-0.5 * hidden_pre * hidden_pre) * inv_root_two_pi
    )


def attend_forward(queries, key_rows, values, key_valid, score_scale):
    length = queries.shape[0]
    block_rows = min(512, length)
    query_blocks = queries.reshape((length // block_rows, block_rows) + queries.shape[1:])

    def one_block(query_block):
        scores = (
            jnp.einsum("qshe,kshe->shqk", query_block, key_rows, preferred_element_type=jnp.float32)
            * score_scale
        )
        scores = jnp.where(key_valid[:, None, None, :], scores, negative_fill)
        row_top = jnp.max(scores, axis=3, keepdims=True)
        exponent = jnp.exp(scores - row_top)
        row_total = jnp.sum(exponent, axis=3, keepdims=True)
        probs_low = (exponent / row_total).astype(jnp.bfloat16)
        context = jnp.einsum(
            "shqk,kshe->qshe", probs_low, values, preferred_element_type=jnp.float32
        )
        return (context.astype(jnp.bfloat16), (row_top + jnp.log(row_total))[..., 0])

    context, lse_rows = lax.map(one_block, query_blocks)
    return (context.reshape(queries.shape), lse_rows)


def attend_backward(queries, key_rows, values, grad_context, lse_rows, key_valid, score_scale):
    length = queries.shape[0]
    block_rows = min(512, length)
    block_shape = (length // block_rows, block_rows) + queries.shape[1:]

    def one_block(carry, pieces):
        grad_keys, grad_values = carry
        query_block, grad_block, lse_block = pieces
        scores = (
            jnp.einsum("qshe,kshe->shqk", query_block, key_rows, preferred_element_type=jnp.float32)
            * score_scale
        )
        scores = jnp.where(key_valid[:, None, None, :], scores, negative_fill)
        probs = jnp.exp(scores - lse_block[..., None])
        grad_values = grad_values + jnp.einsum(
            "shqk,qshe->kshe",
            probs.astype(jnp.bfloat16),
            grad_block,
            preferred_element_type=jnp.float32,
        )
        grad_probs = jnp.einsum(
            "qshe,kshe->shqk", grad_block, values, preferred_element_type=jnp.float32
        )
        inner = jnp.sum(probs * grad_probs, axis=3, keepdims=True)
        grad_scores = (probs * (grad_probs - inner) * score_scale).astype(jnp.bfloat16)
        grad_query = jnp.einsum(
            "shqk,kshe->qshe", grad_scores, key_rows, preferred_element_type=jnp.float32
        )
        grad_keys = grad_keys + jnp.einsum(
            "shqk,qshe->kshe", grad_scores, query_block, preferred_element_type=jnp.float32
        )
        return ((grad_keys, grad_values), grad_query)

    zero_rows = jnp.zeros(key_rows.shape, jnp.float32)
    pieces = (queries.reshape(block_shape), grad_context.reshape(block_shape), lse_rows)
    (grad_keys, grad_values), grad_queries = lax.scan(one_block, (zero_rows, zero_rows), pieces)
    return (grad_queries.reshape(queries.shape), grad_keys, grad_values)


def local(
    tokens,
    cotangent,
    lengths,
    deal_order,
    attn_in,
    attn_out,
    ffn_in,
    ffn_out,
    attn_bias,
    ffn_bias,
    norm_gain,
    shifts,
):
    group_count = lax.axis_size("dp")
    local_seqs = tokens.shape[2] // group_count
    dealt_tokens = jnp.take(tokens, deal_order, axis=2)
    dealt_cot = jnp.take(cotangent, deal_order, axis=2)
    arrived, arrived_cot = (
        lax.all_to_all(dealt_tokens, "dp", split_axis=2, concat_axis=1, tiled=True),
        lax.all_to_all(dealt_cot, "dp", split_axis=2, concat_axis=1, tiled=True),
    )
    half_len = arrived.shape[1]
    model_width = arrived.shape[3]
    tensor_size = lax.axis_size("mp")
    tensor_rank = lax.axis_index("mp")
    seq_len = half_len * tensor_size
    local_rows = half_len * local_seqs
    own_seqs = lax.dynamic_slice_in_dim(deal_order, lax.axis_index("dp") * local_seqs, local_seqs)
    own_lengths = jnp.take(lengths, own_seqs)
    key_valid = jnp.arange(seq_len, dtype=jnp.int32)[None, :] < own_lengths[:, None]
    head_cols = attn_in.shape[3]
    hidden_cols = ffn_in.shape[2]
    head_count = head_cols // HEAD_DIM
    score_scale = HEAD_DIM ** (-0.5)
    layers_total = norm_gain.shape[0]
    shaped = (seq_len, local_seqs, head_count, HEAD_DIM)
    flat_shape = (seq_len * local_seqs, head_cols)

    def layer_vectors(which_layer):
        bias_pair = lax.dynamic_slice_in_dim(
            attn_bias[which_layer].astype(jnp.float32), tensor_rank * head_cols, head_cols, 1
        )
        bias_up = lax.dynamic_slice_in_dim(
            ffn_bias[which_layer].astype(jnp.float32), tensor_rank * hidden_cols, hidden_cols, 0
        )
        return (
            bias_pair,
            bias_up,
            norm_gain[which_layer].astype(jnp.float32),
            shifts[which_layer].astype(jnp.float32),
        )

    hidden_rows = arrived.reshape(local_rows, model_width).astype(jnp.float32)
    weights_all = []
    which_layer = 0
    w_three, w_back, w_up, w_down = fetch_weights(
        attn_in[which_layer], attn_out[which_layer], ffn_in[which_layer], ffn_out[which_layer]
    )
    bias_pair, bias_up, gain_pair, shift_four = layer_vectors(which_layer)
    wide_rows = gather_rows(hidden_rows.astype(jnp.bfloat16))
    projected = jnp.einsum("rd,cde->cre", wide_rows, w_three, preferred_element_type=jnp.float32)
    queries = (projected[0] + bias_pair[0]).astype(jnp.bfloat16).reshape(shaped)
    key_rows = projected[1].astype(jnp.bfloat16).reshape(shaped)
    values = (projected[2] + bias_pair[1]).astype(jnp.bfloat16).reshape(shaped)
    context, lse_rows = attend_forward(queries, key_rows, values, key_valid, score_scale)
    context_rows = context.reshape(flat_shape)

    def attn_term(offset, number, context_rows=context_rows, w_back=w_back):
        return jnp.dot(context_rows, w_back, preferred_element_type=jnp.float32)

    mixed_one = hidden_rows + spread_rows(attn_term, local_rows) + shift_four[0]
    middle, mid_normed, mid_rstd = norm_forward(mixed_one, gain_pair[0], shift_four[1])
    wide_mid = gather_rows(middle.astype(jnp.bfloat16))
    hidden_pre = jnp.dot(wide_mid, w_up, preferred_element_type=jnp.float32) + bias_up
    hidden_low = gelu_value(hidden_pre).astype(jnp.bfloat16)

    def ffn_term(offset, number, hidden_low=hidden_low, w_down=w_down):
        return jnp.dot(hidden_low, w_down, preferred_element_type=jnp.float32)

    mixed_two = middle + spread_rows(ffn_term, local_rows) + shift_four[2]
    hidden_rows, out_normed, out_rstd = norm_forward(mixed_two, gain_pair[1], shift_four[3])
    saved_all = [
        (
            wide_rows,
            queries,
            key_rows,
            values,
            context,
            lse_rows,
            mid_normed,
            mid_rstd,
            wide_mid,
            hidden_pre,
            hidden_low,
            out_normed,
            out_rstd,
        )
    ]
    weights_all.append((w_three, w_back, w_up, w_down))
    grad_state = arrived_cot.reshape(local_rows, model_width).astype(jnp.float32)
    matrix_grads = [None] * layers_total
    attn_bias_parts = [None] * layers_total
    ffn_bias_parts = [None] * layers_total
    gain_parts = [None] * layers_total
    shift_parts = [None] * layers_total
    for which_layer in reversed(range(layers_total)):
        w_three, w_back, w_up, w_down = fetch_again(
            attn_in[which_layer], attn_out[which_layer], ffn_in[which_layer], ffn_out[which_layer]
        )
        bias_pair, bias_up, gain_pair, shift_four = layer_vectors(which_layer)
        (
            wide_rows,
            queries,
            key_rows,
            values,
            context,
            lse_rows,
            mid_normed,
            mid_rstd,
            wide_mid,
            hidden_pre,
            hidden_low,
            out_normed,
            out_rstd,
        ) = saved_all[which_layer]
        grad_mixed_two, grad_gain_two, grad_shift_four = norm_backward(
            grad_state, out_normed, out_rstd, gain_pair[1]
        )
        grad_down_bias = jnp.sum(grad_mixed_two, axis=0)
        grad_down_wide = gather_grads(grad_mixed_two.astype(jnp.bfloat16))
        grad_w_down = contract_rows(hidden_low, grad_down_wide)
        grad_hidden = contract_cols(grad_down_wide, w_down) * gelu_slope(hidden_pre)
        grad_up_bias = jnp.sum(grad_hidden, axis=0)
        grad_hidden_low = grad_hidden.astype(jnp.bfloat16)
        grad_w_up = contract_rows(wide_mid, grad_hidden_low)

        def up_term(offset, number, grad_hidden_low=grad_hidden_low, w_up=w_up):
            return contract_cols(grad_hidden_low, w_up)

        grad_middle = grad_mixed_two + spread_grads(up_term, local_rows)
        grad_mixed_one, grad_gain_one, grad_shift_two = norm_backward(
            grad_middle, mid_normed, mid_rstd, gain_pair[0]
        )
        grad_out_bias = jnp.sum(grad_mixed_one, axis=0)
        grad_attn_wide = gather_grads(grad_mixed_one.astype(jnp.bfloat16))
        context_rows = context.reshape(flat_shape)
        grad_w_back = contract_rows(context_rows, grad_attn_wide)
        grad_context = contract_cols(grad_attn_wide, w_back).astype(jnp.bfloat16).reshape(shaped)
        grad_queries, grad_keys, grad_values = attend_backward(
            queries, key_rows, values, grad_context, lse_rows, key_valid, score_scale
        )
        grad_queries = grad_queries.reshape(flat_shape)
        grad_keys = grad_keys.reshape(flat_shape)
        grad_values = grad_values.reshape(flat_shape)
        grad_pair = jnp.stack([jnp.sum(grad_queries, axis=0), jnp.sum(grad_values, axis=0)])
        grad_projected = jnp.stack([grad_queries, grad_keys, grad_values]).astype(jnp.bfloat16)
        grad_w_three = jnp.einsum(
            "rd,cre->cde", wide_rows, grad_projected, preferred_element_type=jnp.float32
        )

        def three_term(offset, number, grad_projected=grad_projected, w_three=w_three):
            return jnp.einsum(
                "cre,cde->rd", grad_projected, w_three, preferred_element_type=jnp.float32
            )

        grad_state = grad_mixed_one + spread_grads(three_term, local_rows)
        matrix_grads[which_layer] = (
            lax.psum_scatter(grad_w_three, "dp", scatter_dimension=1, tiled=True),
            lax.psum_scatter(grad_w_back, "dp", scatter_dimension=1, tiled=True),
            lax.psum_scatter(grad_w_up, "dp", scatter_dimension=0, tiled=True),
            lax.psum_scatter(grad_w_down, "dp", scatter_dimension=1, tiled=True),
        )
        attn_bias_parts[which_layer] = lax.dynamic_update_slice_in_dim(
            jnp.zeros((2, model_width), jnp.float32), grad_pair, tensor_rank * head_cols, 1
        )
        ffn_bias_parts[which_layer] = lax.dynamic_update_slice_in_dim(
            jnp.zeros((hidden_cols * tensor_size,), jnp.float32),
            grad_up_bias,
            tensor_rank * hidden_cols,
            0,
        )
        gain_parts[which_layer] = jnp.stack([grad_gain_one, grad_gain_two])
        shift_parts[which_layer] = jnp.stack(
            [grad_out_bias, grad_shift_two, grad_down_bias, grad_shift_four]
        )
    three_out, back_out, up_out, down_out = [
        jnp.stack([entry[member] for entry in matrix_grads]) for member in range(4)
    ]
    attn_bias_out, ffn_bias_out, gain_out, shift_out = lax.psum(
        (
            jnp.stack(attn_bias_parts),
            jnp.stack(ffn_bias_parts),
            jnp.stack(gain_parts),
            jnp.stack(shift_parts),
        ),
        ("dp", "mp"),
    )
    result_rows = hidden_rows.astype(jnp.bfloat16).reshape(1, half_len, local_seqs, model_width)
    result_grad = grad_state.astype(jnp.bfloat16).reshape(1, half_len, local_seqs, model_width)
    out_tokens, out_grad = (
        lax.all_to_all(result_rows, "dp", split_axis=1, concat_axis=2, tiled=True),
        lax.all_to_all(result_grad, "dp", split_axis=1, concat_axis=2, tiled=True),
    )
    return (
        out_tokens,
        out_grad,
        three_out,
        back_out,
        up_out,
        down_out,
        attn_bias_out,
        ffn_bias_out,
        gain_out,
        shift_out,
    )


def solution(mesh):
    placed = (
        P("mp", "dp", None, None),
        P("mp", "dp", None, None),
        P(),
        P(),
        P(None, None, "dp", "mp"),
        P(None, "mp", "dp"),
        P(None, "dp", "mp"),
        P(None, "mp", "dp"),
        P(),
        P(),
        P(),
        P(),
    )
    return jax.shard_map(
        local,
        mesh=mesh,
        in_specs=placed,
        out_specs=(
            P("mp", "dp", None, None),
            P("mp", "dp", None, None),
            P(None, None, "dp", "mp"),
            P(None, "mp", "dp"),
            P(None, "dp", "mp"),
            P(None, "mp", "dp"),
            P(),
            P(),
            P(),
            P(),
        ),
        check_vma=False,
    )
```

profile of v0, /device:TPU:0, one launch (start us, length us, event | category | flops | bytes accessed | tf_op | source)
XLA Modules:
  0.0 1211.0 jit_solution(1221424867472361412)
XLA Ops:
  12.6 29.6 %all_to_all.60 = bf16[1,32,16,768]{3,1,0,2:T(8,128)(2,1)} all-to-all(bf16[1,32,16,768]{3,1,0,2:T(8,128)(2,1)S(1)} %get-tuple-element.321), channel_id=1, replica_groups=mesh['dp'=16,'mp'=2] {'dp'}, dimensions={2} | all-to-all | bytes 1572864 | tf_op jit(solution)/shard_map/all_to_all | solution.py:181
  47.0 44.4 %all-gather.1 = bf16[1,384,768]{1,2,0:T(8,128)(2,1)} all-gather(bf16[1,384,48]{1,2,0:T(8,128)(2,1)S(1)} %copy-done.25), channel_id=3, replica_groups=mesh['dp'=16,'mp'=2] {'dp'}, dimensions={2}, use_global_device_ids=true | all-gather | bytes 626688 | tf_op jit(solution)/shard_map/all_gather | solution.py:44
  91.5 22.1 %all-gather.20.cloned.1.call-done = bf16[1,3,768,384]{3,2,1,0:T(8,128)(2,1)} async-done(((bf16[1,3,48,384]{3,2,1,0:T(8,128)(2,1)}), bf16[1,3,768,384]{3,2,1,0:T(8,128)(2,1)}) %all-gather.20.cloned.1.call-update) | async-done | bytes 1769488 | tf_op jit(solution)/shard_map/all_gather | solution.py:43
  123.9 18.0 %while.29 = (s32[]{:T(128)}, bf16[2,512,1,6,64]{1,4,3,2,0:T(8,128)(2,1)S(1)}, f32[2,1,6,512]{3,2,1,0:T(8,128)S(1)}, bf16[2,512,1,6,64]{1,4,3,2,0:T(8,128)(2,1)S(...) while((s32[]{:T(128)}, ...), condition=%wide.region_3.5_spmd.clone, body=%wide.region_0.4_spmd.clone.sunk | while | flops 843249664 | bytes 40231020 | solution.py:119
  158.1 62.5 %all-gather.22.cloned.1.call-done = bf16[1,768,1536]{2,1,0:T(8,128)(2,1)} async-done(((bf16[1,48,1536]{2,1,0:T(8,128)(2,1)}), bf16[1,768,1536]{2,1,0:T(8,128)(2,1)}) %all-gather.22.cloned.1.call-update) | async-done | bytes 2359312 | tf_op jit(solution)/shard_map/all_gather | solution.py:45
  220.6 10.7 all-gather.14.cloned.1.call-done
  238.4 59.4 %all-gather.24.cloned.1.call-done = bf16[1,1536,768]{1,2,0:T(8,128)(2,1)} async-done(((bf16[1,1536,48]{1,2,0:T(8,128)(2,1)}), bf16[1,1536,768]{1,2,0:T(8,128)(2,1)}) %all-gather.24.cloned.1.call-update) | async-done | bytes 2359312 | tf_op jit(solution)/shard_map/all_gather | solution.py:46
  304.4 25.7 %all_to_all.61 = bf16[1,32,16,768]{3,1,0,2:T(8,128)(2,1)S(1)} all-to-all(bf16[1,32,16,768]{3,1,0,2:T(8,128)(2,1)} %get-tuple-element.320), channel_id=1, replica_groups=mesh['dp'=16,'mp'=2] {'dp'}, dimensions={2} | all-to-all | bytes 1572864 | tf_op jit(solution)/shard_map/all_to_all | solution.py:182
  338.0 7.7 all-gather.16.cloned.1.call-done
  345.7 7.7 fusion.141
  358.9 10.3 reduce-scatter.12.cloned.1.call-done
  376.3 11.1 all-gather.18.cloned.1.call-done
  392.7 163.6 %while.30 = (s32[]{:T(128)}, f32[1024,1,6,64]{0,3,2,1:T(8,128)}, f32[1024,1,6,64]{0,3,2,1:T(8,128)}, f32[2,512,1,6,64]{1,4,3,2,0:T(8,128)}, bf16[2,512,1,6,64]{1...) while((s32[]{:T(128)}, f32[1024,1,6,64]{0,3,2,1:T(8,128)}, ...), condition=%wide.region_17.19_spmd.clone, body=%wide.region_15.18_spmd.clone.sunk | while | flops 2096636928 | bytes 199866560 | solution.py:158
  406.1 34.3 %bitcast_add_fusion.4 = f32[1024,1,6,64]{0,3,2,1:T(8,128)} fusion(f32[1024,1,6,64]{0,3,2,1:T(8,128)} %get-tuple-element.475, f32[6,512,1024]{2,1,0:T(8,128)} %fusion.187, f32[6,512,1024]{2,1,0:T(8,128)} %copy-done, f32[6,512]{1,0:T(8,128)S(1)} %dynamic-slice_bitcast_fusion.3, pred[1024]{0:T(1024)(128)(4,1)S(1)} %compare_reduce_fusion.5, ...), kind=kOutput, calls=%fused_computation.42.clone.1 | convolution fusion | flops 438046720 | bytes 53905412 | tf_op jit(solution)/shard_map/while/body/eval_jaxpr/shqk,qshe->kshe/dot_general | solution.py:151
  440.4 33.6 %fusion.189 = f32[2,512,1,6,64]{1,4,3,2,0:T(8,128)} fusion(f32[2,512,1,6,64]{1,4,3,2,0:T(8,128)} %get-tuple-element.477, s32[]{:T(128)S(6)} %copy.127, f32[6,512,1024]{2,1,0:T(8,128)} %fusion.187, f32[6,512,1024]{2,1,0:T(8,128)} %copy-done, f32[6,512]{1,0:T(8,128)S(1)} %dynamic-slice_bitcast_fusion.3, pred[1024]{0:T(1024)(128)(4,1)S(1)} %compare_reduce_fusion.5, ...), kind=kOutput, calls=%fused_computation.44.clone.1 | convolution fusion | flops 437260288 | bytes 51939332 | tf_op jit(solution)/shard_map/while/body/eval_jaxpr/shqk,kshe->qshe/dot_general | solution.py:148
  488.0 34.5 %bitcast_add_fusion.4 = f32[1024,1,6,64]{0,3,2,1:T(8,128)} fusion(f32[1024,1,6,64]{0,3,2,1:T(8,128)} %get-tuple-element.475, f32[6,512,1024]{2,1,0:T(8,128)} %fusion.187, f32[6,512,1024]{2,1,0:T(8,128)} %copy-done, f32[6,512]{1,0:T(8,128)S(1)} %dynamic-slice_bitcast_fusion.3, pred[1024]{0:T(1024)(128)(4,1)S(1)} %compare_reduce_fusion.5, ...), kind=kOutput, calls=%fused_computation.42.clone.1 | convolution fusion | flops 438046720 | bytes 53905412 | tf_op jit(solution)/shard_map/while/body/eval_jaxpr/shqk,qshe->kshe/dot_general | solution.py:151
  522.6 33.6 %fusion.189 = f32[2,512,1,6,64]{1,4,3,2,0:T(8,128)} fusion(f32[2,512,1,6,64]{1,4,3,2,0:T(8,128)} %get-tuple-element.477, s32[]{:T(128)S(6)} %copy.127, f32[6,512,1024]{2,1,0:T(8,128)} %fusion.187, f32[6,512,1024]{2,1,0:T(8,128)} %copy-done, f32[6,512]{1,0:T(8,128)S(1)} %dynamic-slice_bitcast_fusion.3, pred[1024]{0:T(1024)(128)(4,1)S(1)} %compare_reduce_fusion.5, ...), kind=kOutput, calls=%fused_computation.44.clone.1 | convolution fusion | flops 437260288 | bytes 51939332 | tf_op jit(solution)/shard_map/while/body/eval_jaxpr/shqk,kshe->qshe/dot_general | solution.py:148
  622.8 22.3 %all-to-all-done.1 = bf16[16,2,12288]{2,1,0:T(2,128)(2,1)S(1)} async-done(((bf16[16,2,12288]{2,1,0:T(2,128)(2,1)}), bf16[16,2,12288]{2,1,0:T(2,128)(2,1)S(1)}, u32[]{:S(2)}, u32[]{:S(2)}) %all-to-all-start.1) | async-done | bytes 786464 | tf_op jit(solution)/shard_map/all_to_all | solution.py:363
  645.1 9.7 all-to-all-start.3
  658.8 46.7 %all-reduce.1 = (f32[1,2,768]{2,1,0:T(2,128)}, f32[1,3072]{1,0:T(1,128)}, f32[1,2,768]{2,1,0:T(2,128)}, f32[1,4,768]{2,1,0:T(4,128)}) all-reduce(f32[1,2,768]{2,1,0:T(2,128)S(1)} %fusion.130, f32[1,3072]{1,0:T(1,128)S(1)} %reshape_dynamic-update-slice_fusion, ...), channel_id=1, replica_groups=mesh['dp'=16,'mp'=2] {'dp','mp'}, use_global_device_ids=true, to_apply=%region_25.27 | all-reduce | flops 9216 | bytes 73728 | tf_op jit(solution)/shard_map/psum | solution.py:351
  705.5 85.9 %all-reduce.4.cloned.1.call-done = f32[3,768,384]{2,0,1:T(4,128)} async-done(((f32[3,768,384]{2,0,1:T(4,128)}), f32[3,768,384]{2,0,1:T(4,128)}) %all-reduce.4.cloned.1.call-update) | async-done | bytes 3538960
  795.3 124.7 %reduce-scatter.16.cloned.1.call-done = f32[384,48]{0,1:T(8,128)} async-done(((f32[384,768]{0,1:T(8,128)}), f32[384,48]{0,1:T(8,128)}) %reduce-scatter.16.cloned.1.call-update) | async-done | bytes 73744 | tf_op jit(solution)/shard_map/reduce_scatter | solution.py:331
  920.1 142.5 %reduce-scatter.20.cloned.1.call-done = f32[1536,48]{0,1:T(8,128)} async-done(((f32[1536,768]{0,1:T(8,128)}), f32[1536,48]{0,1:T(8,128)}) %reduce-scatter.20.cloned.1.call-update) | async-done | bytes 294928 | tf_op jit(solution)/shard_map/reduce_scatter | solution.py:333
  1062.6 141.7 %reduce-scatter.18.cloned.1.call-done = f32[48,1536]{1,0:T(8,128)} async-done(((f32[768,1536]{1,0:T(8,128)}), f32[48,1536]{1,0:T(8,128)}) %reduce-scatter.18.cloned.1.call-update) | async-done | bytes 294928 | tf_op jit(solution)/shard_map/reduce_scatter | solution.py:332
  (245 shorter events, 191.5 us)
Async XLA Ops:
  7.2 84.3 %all-gather.12.cloned.1.call-start = ((), (), s32[]{:S(2)}) async-start(), calls=%async_computation.11 | async-start | bytes 2359296 | tf_op jit(solution)/shard_map/all_gather | solution.py:16
  12.5 30.5 %copy-start.38 = (s32[16]{0:T(128)S(1)}, s32[16]{0:T(128)}, u32[]{:S(2)}) copy-start(s32[16]{0:T(128)} %param.21) | copy-start | bytes 196
  12.5 33.0 %copy-start.35 = (bf16[1,2,768]{2,1,0:T(2,128)(2,1)S(1)}, bf16[1,2,768]{2,1,0:T(2,128)(2,1)}, u32[]{:S(2)}) copy-start(bf16[1,2,768]{2,1,0:T(2,128)(2,1)} %param.26) | copy-start | bytes 9220
  12.5 33.2 %copy-start.39 = (s32[16]{0:T(128)S(1)}, s32[16]{0:T(128)}, u32[]{:S(2)}) copy-start(s32[16]{0:T(128)} %param.20) | copy-start | bytes 196
  12.5 34.5 %copy-start.25 = (bf16[1,384,48]{1,2,0:T(8,128)(2,1)S(1)}, bf16[1,384,48]{1,2,0:T(8,128)(2,1)}, u32[]{:S(2)}) copy-start(bf16[1,384,48]{1,2,0:T(8,128)(2,1)} %param.23) | copy-start | bytes 110596
  42.2 71.4 %all-gather.20.cloned.1.call-start = ((), (), s32[]{:S(2)}) async-start(), calls=%async_computation.22 | async-start | bytes 1880064 | tf_op jit(solution)/shard_map/all_gather | solution.py:43
  43.0 111.0 %reduce-scatter.8.cloned.1.call-start = ((), (), s32[]{:S(2)}) async-start(), calls=%async_computation.12 | async-start | bytes 2359296 | tf_op jit(solution)/shard_map/reduce_scatter | solution.py:24
  146.0 74.5 %all-gather.22.cloned.1.call-start = ((), (), s32[]{:S(2)}) async-start(), calls=%async_computation.23 | async-start | bytes 2506752 | tf_op jit(solution)/shard_map/all_gather | solution.py:45
  146.6 84.7 %all-gather.14.cloned.1.call-start = ((), (), s32[]{:S(2)}) async-start(), calls=%async_computation.13 | async-start | bytes 2359296 | tf_op jit(solution)/shard_map/all_gather | solution.py:16
  157.4 140.4 %all-gather.24.cloned.1.call-start = ((), (), s32[]{:S(2)}) async-start(), calls=%async_computation.24 | async-start | bytes 2506752 | tf_op jit(solution)/shard_map/all_gather | solution.py:46
  158.0 173.3 %reduce-scatter.10.cloned.1.call-start = ((), (), s32[]{:S(2)}) async-start(), calls=%async_computation.14 | async-start | bytes 2359296 | tf_op jit(solution)/shard_map/reduce_scatter | solution.py:24
  304.3 41.4 %all-gather.16.cloned.1.call-start = ((), (), s32[]{:S(2)}) async-start(), calls=%async_computation.15 | async-start | bytes 2359296 | tf_op jit(solution)/shard_map/all_gather | solution.py:20
  338.0 31.3 %reduce-scatter.12.cloned.1.call-start = ((), (), s32[]{:S(2)}) async-start(), calls=%async_computation.16 | async-start | bytes 2359296 | tf_op jit(solution)/shard_map/reduce_scatter | solution.py:33
  358.9 28.5 %all-gather.18.cloned.1.call-start = ((), (), s32[]{:S(2)}) async-start(), calls=%async_computation.17 | async-start | bytes 2359296 | tf_op jit(solution)/shard_map/all_gather | solution.py:20
  376.2 237.5 %reduce-scatter.14.cloned.1.call-start = ((), (), s32[]{:S(2)}) async-start(), calls=%async_computation.18 | async-start | bytes 2359296 | tf_op jit(solution)/shard_map/reduce_scatter | solution.py:33
  569.5 222.0 %all-reduce.4.cloned.1.call-start = ((), (), s32[]{:S(2)}) async-start(), calls=%async_computation.25 | async-start | bytes 9437184
  577.8 342.2 %reduce-scatter.16.cloned.1.call-start = ((), (), s32[]{:S(2)}) async-start(), calls=%async_computation.19 | async-start | bytes 1253376 | tf_op jit(solution)/shard_map/reduce_scatter | solution.py:331
  582.5 480.1 %reduce-scatter.20.cloned.1.call-start = ((), (), s32[]{:S(2)}) async-start(), calls=%async_computation.21 | async-start | bytes 5013504 | tf_op jit(solution)/shard_map/reduce_scatter | solution.py:333
  588.9 615.4 %reduce-scatter.18.cloned.1.call-start = ((), (), s32[]{:S(2)}) async-start(), calls=%async_computation.20 | async-start | bytes 5013504 | tf_op jit(solution)/shard_map/reduce_scatter | solution.py:332
  606.8 38.3 %all-to-all-start.1 = ((bf16[16,2,12288]{2,1,0:T(2,128)(2,1)}), bf16[16,2,12288]{2,1,0:T(2,128)(2,1)S(1)}, u32[]{:S(2)}, u32[]{:S(2)}) async-start(bf16[16,2,12288]{2,1,0:T(2,128)(2,1)} %reshape.397), calls=%async_computation.3 | async-start | bytes 1572864 | tf_op jit(solution)/shard_map/all_to_all | solution.py:363
  621.6 33.1 %copy-start.40 = (u32[32]{0:T(128)S(1)}, u32[32]{0:T(128)}, u32[]{:S(2)}) copy-start(u32[32]{0:T(128)} %constant.142) | copy-start | bytes 388
  621.7 34.3 %copy-start.7 = (bf16[1,32,16,768]{3,1,0,2:T(8,128)(2,1)S(1)}, bf16[1,32,16,768]{3,1,0,2:T(8,128)(2,1)}, u32[]{:S(2)}) copy-start(bf16[1,32,16,768]{3,1,0,2:T(8,128)(2,1)} %copy-done.5) | copy-start | bytes 2359300
  622.8 33.4 %copy-start.26 = (f32[768]{0:T(1024)S(1)}, f32[768]{0:T(1024)}, u32[]{:S(2)}) copy-start(f32[768]{0:T(1024)} %get-tuple-element.255) | copy-start | bytes 9220
  645.1 148.1 %all-to-all-start.3 = ((bf16[16,2,12288]{2,1,0:T(2,128)(2,1)}), bf16[16,2,12288]{2,1,0:T(2,128)(2,1)S(1)}, u32[]{:S(2)}, u32[]{:S(2)}) async-start(bf16[16,2,12288]{2,1,0:T(2,128)(2,1)} %reshape.399), calls=%async_computation.7 | async-start | bytes 1572864 | tf_op jit(solution)/shard_map/all_to_all | solution.py:364
  (35 other events, 106.2 us)
Sparse Core Ops, SparseCore 0:
  42.3 7.5 all-gather.11
  52.6 60.9 all-gather.19
  146.1 7.8 reduce-scatter.7
  157.0 63.4 all-gather.21
  222.6 8.6 all-gather.13
  234.3 63.4 all-gather.23
  304.4 7.8 reduce-scatter.9
  338.1 7.5 all-gather.15
  359.0 10.2 reduce-scatter.11
  376.3 10.9 all-gather.17
  569.6 10.1 reduce-scatter.13
  585.4 205.9 all-reduce.3
  797.5 122.5 reduce-scatter.15
  926.5 136.0 reduce-scatter.19
  1068.2 136.0 reduce-scatter.17
where the time goes:
time: 1220 us; the launch traced here: 1210 us
  waiting for transfers between devices  710 us (58%)
  matrix products  234 us (19%)
  blocking collectives  147 us (12%)
  other arithmetic  42.7 us (4%)
  local copies, waits for them, and re-layouts  41.3 us (3%)
  between operations  18.2 us (1%)
  starting transfers between devices  17.6 us (1%)
    reduce_scatter x1, waiting for transfers between devices, local(): lax.psum_scatter(grad_w_down, 'dp', scatter_dimension=1, tiled=True)  143 us
    reduce_scatter x1, waiting for transfers between devices, local(): lax.psum_scatter(grad_w_up, 'dp', scatter_dimension=0, tiled=True)  142 us
    reduce_scatter x1, waiting for transfers between devices, local(): lax.psum_scatter(grad_w_back, 'dp', scatter_dimension=1, tiled=True)  125 us
    unnamed x16, waiting for transfers between devices  87.9 us
    dot_general x2, matrix products, one_block(): jnp.einsum('shqk,qshe->kshe', grad_scores, query_block, preferred_element...  68.8 us
    dot_general x2, matrix products, one_block(): jnp.einsum('shqk,kshe->qshe', grad_scores, key_rows, preferred_element_ty...  67.1 us
    all_gather x1, waiting for transfers between devices, fetch_weights(): lax.all_gather(up_part, 'dp', axis=0, tiled=True)  62.5 us
    all_gather x1, waiting for transfers between devices, fetch_weights(): lax.all_gather(down_part, 'dp', axis=1, tiled=True)  59.4 us
  transfers between devices with their start and end apart: 17, of which 13 were waited for; matrix products, arithmetic and copies ran while one was open for 5% of the time, Pallas kernels for 0%

commit v1 on v0

v1 whole, which is shorter than its diff:
```python
import functools

import jax
import jax.numpy as jnp
from jax import lax
from jax.experimental import pallas as pl
from jax.experimental.pallas import tpu as pltpu
from jax.sharding import PartitionSpec as P

HEAD_DIM = 64
PAIR = 2 * HEAD_DIM

eps_norm = 1e-12
root_half = 0.7071067811865476
inv_root_two_pi = 0.3989422804014327
negative_fill = -1000000000.0
F32 = jnp.float32
BF16 = jnp.bfloat16


def matmul(a, b):
    return lax.dot_general(a, b, (((1,), (0,)), ((), ())), preferred_element_type=F32)


def matmul_nt(a, b):
    return lax.dot_general(a, b, (((1,), (1,)), ((), ())), preferred_element_type=F32)


def matmul_tn(a, b):
    return lax.dot_general(a, b, (((0,), (0,)), ((), ())), preferred_element_type=F32)


def xor_permute(x, axis, mask):
    n = lax.axis_size(axis)
    return lax.ppermute(x, axis, [(i, i ^ mask) for i in range(n)])


def dp_axes(n):
    bits = n.bit_length() - 1
    out, at = [], 0
    while at < bits:
        width = 1 if at < 2 else min(2, bits - at)
        out.append((at, 1 << width))
        at += width
    return out[::-1]


def stage_gather(x, axis, shift, size):
    return jnp.concatenate(
        [x] + [xor_permute(x, axis, j << shift) for j in range(1, size)], axis=0
    )


def unscramble_kernel(count, order_of, x_ref, o_ref, sems):
    me = lax.axis_index("dp")
    copies = []
    for block in range(count):
        place = lax.bitwise_xor(me, block)
        spot = 0
        for stride, shift, size in order_of:
            spot = spot + stride * lax.bitwise_and(lax.shift_right_logical(place, shift), size - 1)
        copies.append(pltpu.make_async_copy(x_ref.at[spot], o_ref.at[block], sems.at[block]))
    for copy in copies:
        copy.start()
    for copy in copies:
        copy.wait()


def unscramble(x, stages):
    count = x.shape[0]
    strides, stride = [], 1
    for shift, size in stages:
        strides.append((stride, shift, size))
        stride *= size
    return pl.pallas_call(
        functools.partial(unscramble_kernel, count, tuple(strides)),
        out_shape=jax.ShapeDtypeStruct(x.shape, x.dtype),
        in_specs=[pl.BlockSpec(memory_space=pl.ANY)],
        out_specs=pl.BlockSpec(memory_space=pl.ANY),
        scratch_shapes=[pltpu.SemaphoreType.DMA((count,))],
        name="unscramble",
    )(x)


def gather_rows(x, stages):
    y = x[None]
    for shift, size in stages:
        y = stage_gather(y, "dp", shift, size)
    y = unscramble(y, stages)
    return y.reshape(-1, x.shape[1])


def scatter_sum(g, stages, axes):
    me = lax.axis_index("dp")
    sizes = [size for _, size in axes]
    cols = g.shape[1]
    rows = g.shape[0] // lax.axis_size("dp")
    x = g.reshape(tuple(sizes) + (rows, cols))
    left = list(axes)
    for number, (shift, size) in enumerate(stages):
        at = left.index((shift, size))
        coord = lax.bitwise_and(lax.shift_right_logical(me, shift), size - 1)
        parts = []
        for j in range(1, size):
            piece = lax.dynamic_index_in_dim(x, lax.bitwise_xor(coord, j), at, keepdims=False)
            parts.append(xor_permute(piece, "dp", j << shift))
        own = lax.dynamic_index_in_dim(x, coord, at, keepdims=False).astype(F32)
        parts = [own] + [part.astype(F32) for part in parts]
        while len(parts) > 1:
            parts = [parts[i] + parts[i + 1] for i in range(0, len(parts), 2)]
        x = parts[0]
        if number + 1 < len(stages):
            x = x.astype(BF16)
        left.pop(at)
    return x


def sum_all(v, axes):
    v = v + xor_permute(v, "mp", 1)
    for shift, size in reversed(axes):
        parts = [v] + [xor_permute(v, "dp", j << shift) for j in range(1, size)]
        while len(parts) > 1:
            parts = [parts[i] + parts[i + 1] for i in range(0, len(parts), 2)]
        v = parts[0]
    return v


def attend_forward_kernel(block, qkv_ref, bias_ref, ctx_ref, lse_ref):
    length = qkv_ref.shape[0]
    bias = bias_ref[...]
    for head in range(2):
        low = head * HEAD_DIM
        keys = qkv_ref[:, PAIR + low : PAIR + low + HEAD_DIM]
        values_t = qkv_ref[:, 2 * PAIR + low : 2 * PAIR + low + HEAD_DIM].T
        for start in range(0, length, block):
            queries = qkv_ref[start : start + block, low : low + HEAD_DIM]
            scores = matmul_nt(keys, queries) + bias
            top = jnp.max(scores, axis=0, keepdims=True)
            exponent = jnp.exp(scores - top)
            total = jnp.sum(exponent, axis=0, keepdims=True)
            context_t = matmul(values_t, exponent.astype(BF16)) * (1.0 / total)
            ctx_ref[start : start + block, low : low + HEAD_DIM] = context_t.T.astype(BF16)
            lse_ref[0, head : head + 1, start : start + block] = top + jnp.log(total)


def attend_forward(qkv, bias, pairs):
    length = qkv.shape[0]
    return pl.pallas_call(
        functools.partial(attend_forward_kernel, min(256, length)),
        grid=(pairs,),
        out_shape=(
            jax.ShapeDtypeStruct((length, pairs * PAIR), BF16),
            jax.ShapeDtypeStruct((pairs, 2, length), F32),
        ),
        in_specs=[
            pl.BlockSpec((length, 3 * PAIR), lambda p: (0, p)),
            pl.BlockSpec((length, 1), lambda p: (0, 0)),
        ],
        out_specs=(
            pl.BlockSpec((length, PAIR), lambda p: (0, p)),
            pl.BlockSpec((1, 2, length), lambda p: (p, 0, 0)),
        ),
        compiler_params=pltpu.CompilerParams(vmem_limit_bytes=48 << 20),
        cost_estimate=pl.CostEstimate(
            flops=pairs * 2 * 4 * length * length * HEAD_DIM * 8,
            transcendentals=pairs * 2 * length * length,
            bytes_accessed=pairs * length * PAIR * 8,
        ),
        name="attend_forward",
    )(qkv, bias)


def attend_backward_kernel(block, qkv_ref, dctx_ref, lse_ref, bias_ref, out_ref, sums_ref, dk_ref, dv_ref):
    length = qkv_ref.shape[0]
    bias = bias_ref[...]
    for head in range(2):
        low = head * HEAD_DIM
        keys = qkv_ref[:, PAIR + low : PAIR + low + HEAD_DIM]
        keys_t = keys.T
        values = qkv_ref[:, 2 * PAIR + low : 2 * PAIR + low + HEAD_DIM]
        query_sum = jnp.zeros((1, HEAD_DIM), F32)
        for start in range(0, length, block):
            queries = qkv_ref[start : start + block, low : low + HEAD_DIM]
            grads = dctx_ref[start : start + block, low : low + HEAD_DIM]
            lse = lse_ref[0, head : head + 1, start : start + block]
            probs = jnp.exp(matmul_nt(keys, queries) + bias - lse)
            grad_probs = matmul_nt(values, grads)
            inner = jnp.sum(probs * grad_probs, axis=0, keepdims=True)
            grad_scores = (probs * (grad_probs - inner)).astype(BF16)
            dv = matmul(probs.astype(BF16), grads)
            dk = matmul(grad_scores, queries)
            if start == 0:
                dk_ref[...] = dk
                dv_ref[...] = dv
            else:
                dk_ref[...] += dk
                dv_ref[...] += dv
            dq = (matmul(keys_t, grad_scores) * HEAD_DIM ** (-0.5)).T
            query_sum = query_sum + jnp.sum(dq, axis=0, keepdims=True)
            out_ref[start : start + block, low : low + HEAD_DIM] = dq.astype(BF16)
        dk = dk_ref[...]
        dv = dv_ref[...]
        out_ref[:, PAIR + low : PAIR + low + HEAD_DIM] = dk.astype(BF16)
        out_ref[:, 2 * PAIR + low : 2 * PAIR + low + HEAD_DIM] = dv.astype(BF16)
        sums_ref[0, 0:1, low : low + HEAD_DIM] = query_sum
        sums_ref[0, 1:2, low : low + HEAD_DIM] = jnp.sum(dv, axis=0, keepdims=True)


def attend_backward(qkv, dctx, lse, bias, pairs):
    length = qkv.shape[0]
    return pl.pallas_call(
        functools.partial(attend_backward_kernel, min(256, length)),
        grid=(pairs,),
        out_shape=(
            jax.ShapeDtypeStruct((length, pairs * 3 * PAIR), BF16),
            jax.ShapeDtypeStruct((pairs, 2, PAIR), F32),
        ),
        in_specs=[
            pl.BlockSpec((length, 3 * PAIR), lambda p: (0, p)),
            pl.BlockSpec((length, PAIR), lambda p: (0, p)),
            pl.BlockSpec((1, 2, length), lambda p: (p, 0, 0)),
            pl.BlockSpec((length, 1), lambda p: (0, 0)),
        ],
        out_specs=(
            pl.BlockSpec((length, 3 * PAIR), lambda p: (0, p)),
            pl.BlockSpec((1, 2, PAIR), lambda p: (p, 0, 0)),
        ),
        scratch_shapes=[pltpu.VMEM((length, HEAD_DIM), F32), pltpu.VMEM((length, HEAD_DIM), F32)],
        compiler_params=pltpu.CompilerParams(vmem_limit_bytes=48 << 20),
        cost_estimate=pl.CostEstimate(
            flops=pairs * 2 * 10 * length * length * HEAD_DIM * 8,
            transcendentals=pairs * 2 * length * length,
            bytes_accessed=pairs * length * PAIR * 16,
        ),
        name="attend_backward",
    )(qkv, dctx, lse, bias)


def norm_forward(rows):
    center = rows - jnp.mean(rows, axis=1, keepdims=True)
    rstd = lax.rsqrt(jnp.mean(center * center, axis=1, keepdims=True) + eps_norm)
    return center * rstd, rstd


def norm_backward(grad, normed, rstd, gain):
    scaled = grad * gain
    inner = (
        scaled
        - jnp.mean(scaled, axis=1, keepdims=True)
        - normed * jnp.mean(scaled * normed, axis=1, keepdims=True)
    )
    return rstd * inner, jnp.sum(grad * normed, axis=0), jnp.sum(grad, axis=0)


def gelu_value(u):
    return 0.5 * u * (1.0 + lax.erf(u * root_half))


def gelu_slope(u):
    return 0.5 * (1.0 + lax.erf(u * root_half)) + u * jnp.exp(-0.5 * u * u) * inv_root_two_pi


def both_halves(own):
    return jnp.concatenate([own, xor_permute(own, "mp", 1)], axis=0)


def sum_over_mp(part):
    half = part.shape[0] // 2
    other = xor_permute(part.astype(BF16), "mp", 1).astype(F32)
    return part + jnp.concatenate([other[half:], other[:half]], axis=0)


def exchange_in(x, deal_order):
    dealt = jnp.take(x[0], deal_order, axis=1).transpose(1, 0, 2)
    arrived = lax.all_to_all(dealt, "dp", split_axis=0, concat_axis=0, tiled=True)
    return arrived.reshape(-1, x.shape[3])


def exchange_out(rows):
    n = lax.axis_size("dp")
    sent = lax.all_to_all(
        rows.reshape(n, rows.shape[0] // n, rows.shape[1]), "dp", split_axis=0, concat_axis=0, tiled=True
    )
    return sent.transpose(1, 0, 2)[None]


def local(
    tokens, cotangent, lengths, deal_order, attn_in, attn_out, ffn_in, ffn_out,
    attn_bias, ffn_bias, norm_gain, shifts,
):
    dp_size = lax.axis_size("dp")
    mp_rank = lax.axis_index("mp")
    dp_rank = lax.axis_index("dp")
    axes = dp_axes(dp_size)
    low = axes[-2:]
    high = axes[:-2]
    order_one = high + low
    order_two = high + low[::-1]
    back_one = low[::-1] + high[::-1]
    back_two = low + high[::-1]

    width = tokens.shape[3]
    half_len = tokens.shape[1] * dp_size
    seq_len = 2 * half_len
    head_cols = attn_in.shape[3]
    hidden_cols = ffn_in.shape[2]
    pairs = head_cols // PAIR
    shard_rows = attn_in.shape[2]

    three = attn_in[0].reshape(3, shard_rows, pairs, PAIR).transpose(1, 2, 0, 3)
    three = three.reshape(shard_rows, 3 * head_cols)
    back_t = attn_out[0].T
    up = ffn_in[0]
    down_t = ffn_out[0].T
    attn_own = jnp.concatenate([three, back_t], axis=1)
    mid_col = attn_own.shape[1] // 2

    tok_own = exchange_in(tokens, deal_order)
    w_first = gather_rows(attn_own[:, :mid_col], order_one)
    w_second = gather_rows(attn_own[:, mid_col:], order_two)
    w_attn = jnp.concatenate([w_first, w_second], axis=1)
    w_three, w_back = w_attn[:, : 3 * head_cols], w_attn[:, 3 * head_cols :]
    w_up = gather_rows(up, order_one)
    w_down = lax.all_gather(down_t, "dp", axis=0, tiled=True)

    hb = both_halves(tok_own)
    hidden = hb.astype(F32)
    length = lengths[deal_order[dp_rank]]
    place = jnp.arange(seq_len, dtype=jnp.int32)
    place = jnp.where(mp_rank == 0, place, (place + half_len) % seq_len)
    bias_col = jnp.where(place < length, 0.0, negative_fill).astype(F32)[:, None]

    def own_cols(v, count):
        return lax.dynamic_slice_in_dim(v, mp_rank * count, count, v.ndim - 1)

    bias_pair = own_cols(attn_bias[0].astype(F32), head_cols).reshape(2, pairs, PAIR)
    bias_three = jnp.stack([bias_pair[0], jnp.zeros_like(bias_pair[0]), bias_pair[1]], axis=1)
    bias_up = own_cols(ffn_bias[0].astype(F32), hidden_cols)
    scale_three = jnp.concatenate(
        [jnp.full((pairs, 1, PAIR), HEAD_DIM ** (-0.5), F32), jnp.ones((pairs, 2, PAIR), F32)], axis=1
    ).reshape(-1)
    gain = norm_gain[0].astype(F32)
    shift = shifts[0].astype(F32)

    qkv = ((matmul(hb, w_three) + bias_three.reshape(-1)) * scale_three).astype(BF16)
    context, lse = attend_forward(qkv, bias_col, pairs)
    mixed_one = hidden + sum_over_mp(matmul_nt(context, w_back)) + shift[0]
    mid_normed, mid_rstd = norm_forward(mixed_one)
    middle = mid_normed * gain[0] + shift[1]
    mid_low = middle.astype(BF16)
    hidden_pre = matmul(mid_low, w_up) + bias_up
    hidden_low = gelu_value(hidden_pre).astype(BF16)
    mixed_two = middle + sum_over_mp(matmul_nt(hidden_low, w_down)) + shift[2]
    out_normed, out_rstd = norm_forward(mixed_two)
    result = (out_normed[:half_len] * gain[1] + shift[3]).astype(BF16)
    out_tokens = exchange_out(result)

    cot = both_halves(exchange_in(cotangent, deal_order)).astype(F32)
    grad_two, grad_gain_two, grad_shift_four = norm_backward(cot, out_normed, out_rstd, gain[1])
    grad_down_bias = jnp.sum(grad_two, axis=0)
    grad_two_low = grad_two.astype(BF16)
    grad_w_down = matmul_tn(grad_two_low, hidden_low).astype(BF16)
    down_sum = scatter_sum(grad_w_down, back_one, axes)
    grad_hidden = matmul(grad_two_low, w_down) * gelu_slope(hidden_pre)
    grad_up_bias = jnp.sum(grad_hidden, axis=0)
    grad_hidden_low = grad_hidden.astype(BF16)
    grad_w_up = matmul_tn(mid_low, grad_hidden_low).astype(BF16)
    up_sum = scatter_sum(grad_w_up, back_two, axes)
    grad_middle = grad_two + sum_over_mp(matmul_nt(grad_hidden_low, w_up))
    grad_one, grad_gain_one, grad_shift_two = norm_backward(grad_middle, mid_normed, mid_rstd, gain[0])
    grad_out_bias = jnp.sum(grad_one, axis=0)
    grad_one_low = grad_one.astype(BF16)
    grad_w_back = matmul_tn(grad_one_low, context).astype(BF16)
    grad_context = matmul(grad_one_low, w_back).astype(BF16)
    dqkv, pair_sums = attend_backward(qkv, grad_context, lse, bias_col, pairs)
    grad_w_three = matmul_tn(hb, dqkv).astype(BF16)
    grad_attn = jnp.concatenate([grad_w_three, grad_w_back], axis=1)
    first_sum = scatter_sum(grad_attn[:, :mid_col], back_one, axes)
    second_sum = scatter_sum(grad_attn[:, mid_col:], back_two, axes)
    attn_sum = jnp.concatenate([first_sum, second_sum], axis=1)
    grad_part = matmul_nt(dqkv, w_three)
    grad_in = (
        grad_one[:half_len]
        + grad_part[:half_len]
        + xor_permute(grad_part[half_len:].astype(BF16), "mp", 1).astype(F32)
    ).astype(BF16)
    out_grad = exchange_out(grad_in)

    def spread(v, count):
        full = jnp.zeros(v.shape[:-1] + (2 * count,), F32)
        return lax.dynamic_update_slice_in_dim(full, v, mp_rank * count, v.ndim - 1)

    sums_pair = pair_sums.transpose(1, 0, 2).reshape(2, head_cols)
    small = [
        spread(sums_pair, head_cols),
        spread(grad_up_bias, hidden_cols),
        0.5 * jnp.stack([grad_gain_one, grad_gain_two]),
        0.5 * jnp.stack([grad_out_bias, grad_shift_two, grad_down_bias, grad_shift_four]),
    ]
    flat = jnp.concatenate([v.reshape(-1, 128) for v in small], axis=0)
    flat = sum_all(flat, axes)
    outs, at = [], 0
    for v in small:
        rows = v.size // 128
        outs.append(flat[at : at + rows].reshape((1,) + v.shape))
        at += rows
    attn_bias_out, ffn_bias_out, gain_out, shift_out = outs

    three_out = attn_sum[:, : 3 * head_cols].reshape(shard_rows, pairs, 3, PAIR)
    three_out = three_out.transpose(2, 0, 1, 3).reshape(1, 3, shard_rows, head_cols)
    back_out = attn_sum[:, 3 * head_cols :].T[None]
    up_out = up_sum[None]
    down_out = down_sum.T[None]
    return (
        out_tokens, out_grad, three_out, back_out, up_out, down_out,
        attn_bias_out, ffn_bias_out, gain_out, shift_out,
    )


def solution(mesh):
    placed = (
        P("mp", "dp", None, None),
        P("mp", "dp", None, None),
        P(),
        P(),
        P(None, None, "dp", "mp"),
        P(None, "mp", "dp"),
        P(None, "dp", "mp"),
        P(None, "mp", "dp"),
        P(),
        P(),
        P(),
        P(),
    )
    return jax.shard_map(
        local,
        mesh=mesh,
        in_specs=placed,
        out_specs=(
            P("mp", "dp", None, None),
            P("mp", "dp", None, None),
            P(None, None, "dp", "mp"),
            P(None, "mp", "dp"),
            P(None, "dp", "mp"),
            P(None, "mp", "dp"),
            P(),
            P(),
            P(),
            P(),
        ),
        check_vma=False,
    )
```

time: 1220 us -> 582 us (0.48)
  waiting for transfers between devices: 710 us -> 140 us
  matrix products: 234 us -> 45.6 us
  Pallas kernels: 0 us -> 187 us
  blocking collectives: 147 us -> 0 us
  starting transfers between devices: 17.6 us -> 85.4 us
  local copies, waits for them, and re-layouts: 41.3 us -> 62 us
    reduce_scatter x7 -> x0, waiting for transfers between devices: 426 us -> none  [the longest x1 143 us: local(): lax.psum_scatter(grad_w_down, 'dp', scatter_dimension=1, tiled=True)]
    dot_general x26 -> x12, matrix products: 234 us -> 45.6 us  [the longest x4 19.2 us: matmul_nt(): lax.dot_general(a, b, (((1,), (1,)), ((), ())), preferred_element_type=F32)]
    pallas_call x0 -> x5, Pallas kernels: none -> 187 us  [the longest x3 147 us: unscramble(): pl.pallas_call(functools.partial(unscramble_kernel, count, tuple(strides)...]
    all_gather x7 -> x1, waiting for transfers between devices: 173 us -> 0.01 us  [local(): w_down = lax.all_gather(down_t, 'dp', axis=0, tiled=True)]
    ppermute x0 -> x47, waiting for transfers between devices: none -> 120 us  [xor_permute(): return lax.ppermute(x, axis, [(i, i ^ mask) for i in range(n)])]
    unnamed x16 -> x1, waiting for transfers between devices: 87.9 us -> 0.68 us
    ppermute x0 -> x47, starting transfers between devices: none -> 61.5 us  [xor_permute(): return lax.ppermute(x, axis, [(i, i ^ mask) for i in range(n)])]
    all_to_all x2 -> x0, blocking collectives: 55.4 us -> none  [the longest x1 29.6 us: local(): lax.all_to_all(dealt_tokens, 'dp', split_axis=2, concat_axis=1, tiled=True)]
  transfers between devices with their start and end apart: 17 -> 52, of which waited for: 13 -> 16; matrix products, arithmetic and copies ran while one was open for 5% -> 19% of each run, Pallas kernels for 0% -> 32%
where the time goes in v1:
time: 582 us; the launch traced here: 576 us
  Pallas kernels  187 us (32%)
  waiting for transfers between devices  140 us (24%)
  starting transfers between devices  85.4 us (15%)
  local copies, waits for them, and re-layouts  62 us (11%)
  matrix products  45.6 us (8%)
  other arithmetic  38.7 us (7%)
  between operations  17.4 us (3%)
    pallas_call x3, Pallas kernels, unscramble(): pl.pallas_call(functools.partial(unscramble_kernel, count, tuple(strides)...  147 us
    ppermute x47, waiting for transfers between devices, xor_permute(): return lax.ppermute(x, axis, [(i, i ^ mask) for i in range(n)])  120 us
    ppermute x47, starting transfers between devices, xor_permute(): return lax.ppermute(x, axis, [(i, i ^ mask) for i in range(n)])  61.5 us
    unnamed x115, local copies, waits for them, and re-layouts  29.9 us
    pallas_call x1, Pallas kernels, attend_backward(): pl.pallas_call(functools.partial(attend_backward_kernel, min(256, length)...  22.2 us
    all_to_all x2, waiting for transfers between devices, exchange_in(): lax.all_to_all(dealt, 'dp', split_axis=0, concat_axis=0, tiled=True)  20 us
    dot_general x4, matrix products, matmul_nt(): lax.dot_general(a, b, (((1,), (1,)), ((), ())), preferred_element_type=F32)  19.2 us
    pallas_call x1, Pallas kernels, attend_forward(): pl.pallas_call(functools.partial(attend_forward_kernel, min(256, length))...  17.9 us
  transfers between devices with their start and end apart: 52, of which 16 were waited for; matrix products, arithmetic and copies ran while one was open for 19% of the time, Pallas kernels for 32%

profile of v1, /device:TPU:0, one launch (start us, length us, event | category | flops | bytes accessed | tf_op | source)
XLA Modules:
  0.0 576.5 jit_solution(5220666570941292118)
XLA Ops:
  46.3 4.5 collective-permute-done.3
  75.9 26.3 %collective-permute-done.10 = bf16[8,48,768]{2,1,0:T(8,128)(2,1)} collective-permute-done((bf16[8,48,768]{2,1,0:T(8,128)(2,1)}, bf16[8,48,768]{2,1,0:T(8,128)(2,1)}, u32[]{:S(2)}, u32[]{:S(2)}) %collective-permute-start.10) | collective-permute-done | bytes 589856 | tf_op jit(solution)/shard_map/ppermute | solution.py:35
  104.4 37.0 %unscramble.4 = bf16[16,48,768]{2,1,0:T(8,128)(2,1)} custom-call(bf16[16,48,768]{2,1,0:T(8,128)(2,1)} %copy-done.28), custom_call_target="tpu_custom_call" | custom-call | tf_op jit(solution)/shard_map/unscramble/pallas_call | solution.py:75
  143.4 37.0 %unscramble.3 = bf16[16,48,768]{2,1,0:T(8,128)(2,1)} custom-call(bf16[16,48,768]{2,1,0:T(8,128)(2,1)} %constant_dynamic-update-slice_fusion.5.x_ref), custom_call_target="tpu_custom_call" | custom-call | tf_op jit(solution)/shard_map/unscramble/pallas_call | solution.py:75
  184.2 17.9 %attend_forward.1 = (bf16[1024,384]{1,0:T(8,128)(2,1)S(1)}, f32[3,2,1024]{2,1,0:T(2,128)S(1)}) custom-call(bf16[1024,1152]{1,0:T(8,128)(2,1)S(1)} %multiply_convert_fusion.1.qkv_ref, f32[1024,1]{1,0:T(8,128)S(1)} %fusion.43.bias_ref), custom_call_target="tpu_custom_call" | custom-call | flops 12884901888 | bytes 3145728 | tf_op jit(solution)/shard_map/attend_forward/pallas_call | solution.py:148
  209.1 27.1 %collective-permute-done.16 = bf16[8,48,1536]{2,1,0:T(8,128)(2,1)} collective-permute-done((bf16[8,48,1536]{2,1,0:T(8,128)(2,1)}, bf16[8,48,1536]{2,1,0:T(8,128)(2,1)}, u32[]{:S(2)}, u32[]{:S(2)}) %collective-permute-start.16) | collective-permute-done | bytes 1179680 | tf_op jit(solution)/shard_map/ppermute | solution.py:35
  238.6 72.7 %unscramble.5 = bf16[16,48,1536]{2,1,0:T(8,128)(2,1)} custom-call(bf16[16,48,1536]{2,1,0:T(8,128)(2,1)} %constant_dynamic-update-slice_fusion.27.x_ref), custom_call_target="tpu_custom_call" | custom-call | tf_op jit(solution)/shard_map/unscramble/pallas_call | solution.py:75
  317.0 5.7 multiply_convert_fusion
  322.7 7.5 %fusion.80 = (bf16[1024,768]{1,0:T(8,128)(2,1)}, f32[1024,768]{1,0:T(8,128)}) fusion(bf16[1024,1536]{1,0:T(8,128)(2,1)} %get-tuple-element.123, bf16[768,1536]{1,0:T(8,128)(2,1)} %all-gather.2.cloned.1.call-done), kind=kOutput, calls=%fused_computation.224 | convolution fusion | flops 2416705536 | bytes 10223616 | tf_op jit(solution)/shard_map/dot_general | solution.py:26
  330.2 9.6 %all-to-all-start.2 = ((bf16[16,32,768]{2,1,0:T(8,128)(2,1)}), bf16[16,32,768]{2,1,0:T(8,128)(2,1)S(1)}, u32[]{:S(2)}, u32[]{:S(2)}) async-start(bf16[16,32,768]{2,1,0:T(8,128)(2,1)} %get-tuple-element.120), calls=%async_computation.2 | async-start | bytes 1572864 | tf_op jit(solution)/shard_map/all_to_all | solution.py:275
  339.9 20.0 %all-to-all-done.2 = bf16[16,32,768]{2,1,0:T(8,128)(2,1)S(1)} async-done(((bf16[16,32,768]{2,1,0:T(8,128)(2,1)}), bf16[16,32,768]{2,1,0:T(8,128)(2,1)S(1)}, u32[]{:S(2)}, u32[]{:S(2)}) %all-to-all-start.2) | async-done | bytes 786464 | tf_op jit(solution)/shard_map/all_to_all | solution.py:275
  376.3 4.5 fusion.82
  388.1 4.3 fusion.81
  393.4 5.4 all-to-all-start.1
  407.7 15.4 %collective-permute-done.31 = bf16[4,2,48,1536]{3,2,0,1:T(8,128)(2,1)} collective-permute-done((bf16[4,2,48,1536]{3,2,0,1:T(8,128)(2,1)}, bf16[4,2,48,1536]{3,2,0,1:T(8,128)(2,1)}, u32[]{:S(2)}, u32[]{:S(2)}) %collective-permute-start.31) | collective-permute-done | bytes 1179680 | tf_op jit(solution)/shard_map/ppermute | solution.py:35
  433.0 5.0 multiply_reduce_fusion
  438.0 4.6 fusion.64
  445.8 22.2 %attend_backward.1 = (bf16[1024,1152]{1,0:T(8,128)(2,1)S(1)}, f32[3,2,128]{2,1,0:T(2,128)S(1)}) custom-call(bf16[1024,1152]{1,0:T(8,128)(2,1)S(1)} %copy-done.3, bf16[1024,384]{1,0:T(8,128)(2,1)S(1)} %convolution_convert_fusion.3.dctx_ref, f32[3,2,1024]{2,1,0:T(2,128)S(1)} %get-tuple-element.16.lse_ref, f32[1024,1]{1,0:T(8,128)S(1)} %fusion.43.bias_ref), custom_call_target="tpu_custom_call" | custom-call | flops 32212254720 | bytes 6291456 | tf_op jit(solution)/shard_map/attend_backward/pallas_call | solution.py:211
  469.6 4.4 fusion.31
  510.1 5.7 collective-permute-done.39
  518.9 6.4 %collective-permute-done.34 = bf16[48,1536]{1,0:T(8,128)(2,1)S(1)} collective-permute-done((bf16[48,1536]{1,0:T(8,128)(2,1)S(1)}, bf16[48,1536]{1,0:T(8,128)(2,1)S(1)}, u32[]{:S(2)}, u32[]{:S(2)}) %collective-permute-start.34) | collective-permute-done | bytes 147488 | tf_op jit(solution)/shard_map/ppermute | solution.py:35
  531.9 5.1 all-to-all-start.3
  546.0 6.5 %collective-permute-done.23 = bf16[48,768]{1,0:T(8,128)(2,1)S(1)} collective-permute-done((bf16[48,768]{1,0:T(8,128)(2,1)S(1)}, bf16[48,768]{1,0:T(8,128)(2,1)S(1)}, u32[]{:S(2)}, u32[]{:S(2)}) %collective-permute-start.23) | collective-permute-done | bytes 73760 | tf_op jit(solution)/shard_map/ppermute | solution.py:35
  556.4 7.9 %collective-permute-done.24 = bf16[48,768]{1,0:T(8,128)(2,1)S(1)} collective-permute-done((bf16[48,768]{1,0:T(8,128)(2,1)S(1)}, bf16[48,768]{1,0:T(8,128)(2,1)S(1)}, u32[]{:S(2)}, u32[]{:S(2)}) %collective-permute-start.24) | collective-permute-done | bytes 73760 | tf_op jit(solution)/shard_map/ppermute | solution.py:35
  (328 shorter events, 196.4 us)
Async XLA Ops:
  9.9 25.6 %collective-permute-start.6 = (bf16[1,48,768]{2,1,0:T(8,128)(2,1)S(1)}, bf16[1,48,768]{2,1,0:T(8,128)(2,1)S(1)}, u32[]{:S(2)}, u32[]{:S(2)}) collective-permute-start(bf16[1,48,768]{2,1,0:T(8,128)(2,1)S(1)} %get-tuple-element.102), channel_id=1, source_target_pairs={{0,8},{2,10},{4,12},{6,14},{8,0},{10,2},{12,4},{14,6},{16,24},{18,... | collective-permute-start | bytes 221192 | tf_op jit(solution)/shard_map/ppermute | solution.py:35
  12.9 26.4 %collective-permute-start.7 = (bf16[1,48,768]{2,1,0:T(8,128)(2,1)S(1)}, bf16[1,48,768]{2,1,0:T(8,128)(2,1)S(1)}, u32[]{:S(2)}, u32[]{:S(2)}) collective-permute-start(bf16[1,48,768]{2,1,0:T(8,128)(2,1)S(1)} %get-tuple-element.102), channel_id=1, source_target_pairs={{0,16},{2,18},{4,20},{6,22},{8,24},{10,26},{12,28},{14,30},{16,0},... | collective-permute-start | bytes 221192 | tf_op jit(solution)/shard_map/ppermute | solution.py:35
  17.0 27.8 %collective-permute-start.2 = (bf16[1,48,768]{2,1,0:T(8,128)(2,1)}, bf16[1,48,768]{2,1,0:T(8,128)(2,1)S(1)}, u32[]{:S(2)}, u32[]{:S(2)}) collective-permute-start(bf16[1,48,768]{2,1,0:T(8,128)(2,1)} %slice_bitcast_fusion.1), channel_id=1, source_target_pairs={{0,16},{2,18},{4,20},{6,22},{8,24},{10,26},{12,28},{14,30},{16,0},... | collective-permute-start | bytes 221192 | tf_op jit(solution)/shard_map/ppermute | solution.py:35
  26.1 43.8 %all-to-all-start = ((bf16[16,32,768]{2,1,0:T(8,128)(2,1)}), bf16[16,32,768]{2,1,0:T(8,128)(2,1)S(1)}, u32[]{:S(2)}, u32[]{:S(2)}) async-start(bf16[16,32,768]{2,1,0:T(8,128)(2,1)} %get-tuple-element.119), calls=%async_computation | async-start | bytes 1572864 | tf_op jit(solution)/shard_map/all_to_all | solution.py:275
  29.9 292.8 %all-gather.2.cloned.1.call-start = ((), (), s32[]{:S(2)}) async-start(), calls=%async_computation.4 | async-start | bytes 2506752 | tf_op jit(solution)/shard_map/all_gather | solution.py:324
  39.4 26.1 %collective-permute-start.13 = (bf16[1,48,1536]{2,1,0:T(8,128)(2,1)S(1)}, bf16[1,48,1536]{2,1,0:T(8,128)(2,1)S(1)}, u32[]{:S(2)}, u32[]{:S(2)}) collective-permute-start(bf16[1,48,1536]{2,1,0:T(8,128)(2,1)S(1)} %copy-done.34), channel_id=1, source_target_pairs={{0,16},{2,18},{4,20},{6,22},{8,24},{10,26},{12,28},{14,30},{16,0},... | collective-permute-start | bytes 442376 | tf_op jit(solution)/shard_map/ppermute | solution.py:35
  66.4 139.0 %collective-permute-start.15 = (bf16[4,48,1536]{2,1,0:T(8,128)(2,1)}, bf16[4,48,1536]{2,1,0:T(8,128)(2,1)}, u32[]{:S(2)}, u32[]{:S(2)}) collective-permute-start(bf16[4,48,1536]{2,1,0:T(8,128)(2,1)} %pad_maximum_fusion.6), channel_id=1, source_target_pairs={{0,4},{2,6},{4,0},{6,2},{8,12},{10,14},{12,8},{14,10},{16,20},{18,... | collective-permute-start | bytes 1769480 | tf_op jit(solution)/shard_map/ppermute | solution.py:35
  69.5 32.8 %collective-permute-start.10 = (bf16[8,48,768]{2,1,0:T(8,128)(2,1)}, bf16[8,48,768]{2,1,0:T(8,128)(2,1)}, u32[]{:S(2)}, u32[]{:S(2)}) collective-permute-start(bf16[8,48,768]{2,1,0:T(8,128)(2,1)} %get-tuple-element.89), channel_id=1, source_target_pairs={{0,4},{2,6},{4,0},{6,2},{8,12},{10,14},{12,8},{14,10},{16,20},{18,... | collective-permute-start | bytes 1769480 | tf_op jit(solution)/shard_map/ppermute | solution.py:35
  69.9 110.5 %collective-permute-start = (bf16[512,768]{1,0:T(8,128)(2,1)S(1)}, bf16[512,768]{1,0:T(8,128)(2,1)S(1)}, u32[]{:S(2)}, u32[]{:S(2)}) collective-permute-start(bf16[512,768]{1,0:T(8,128)(2,1)S(1)} %bitcast.178), channel_id=1, source_target_pairs={{0,1},{1,0},{2,3},{3,2},{4,5},{5,4},{6,7},{7,6},{8,9},{9,8},{10,11... | collective-permute-start | bytes 2359304 | tf_op jit(solution)/shard_map/ppermute | solution.py:35
  72.0 69.4 %collective-permute-start.5 = (bf16[8,48,768]{2,1,0:T(8,128)(2,1)}, bf16[8,48,768]{2,1,0:T(8,128)(2,1)}, u32[]{:S(2)}, u32[]{:S(2)}) collective-permute-start(bf16[8,48,768]{2,1,0:T(8,128)(2,1)} %get-tuple-element.87), channel_id=1, source_target_pairs={{0,2},{2,0},{4,6},{6,4},{8,10},{10,8},{12,14},{14,12},{16,18},{18,... | collective-permute-start | bytes 1769480 | tf_op jit(solution)/shard_map/ppermute | solution.py:35
  205.3 106.0 %collective-permute-start.11 = (bf16[1024,768]{1,0:T(8,128)(2,1)}, bf16[1024,768]{1,0:T(8,128)(2,1)S(1)}, u32[]{:S(2)}, u32[]{:S(2)}) collective-permute-start(bf16[1024,768]{1,0:T(8,128)(2,1)} %get-tuple-element.121), channel_id=1, source_target_pairs={{0,1},{1,0},{2,3},{3,2},{4,5},{5,4},{6,7},{7,6},{8,9},{9,8},{10,11... | collective-permute-start | bytes 4718600 | tf_op jit(solution)/shard_map/ppermute | solution.py:35
  207.5 28.7 %collective-permute-start.16 = (bf16[8,48,1536]{2,1,0:T(8,128)(2,1)}, bf16[8,48,1536]{2,1,0:T(8,128)(2,1)}, u32[]{:S(2)}, u32[]{:S(2)}) collective-permute-start(bf16[8,48,1536]{2,1,0:T(8,128)(2,1)} %get-tuple-element.79), channel_id=1, source_target_pairs={{0,2},{2,0},{4,6},{6,4},{8,10},{10,8},{12,14},{14,12},{16,18},{18,... | collective-permute-start | bytes 3538952 | tf_op jit(solution)/shard_map/ppermute | solution.py:35
  330.2 29.7 %collective-permute-start.17 = (bf16[1024,768]{1,0:T(8,128)(2,1)}, bf16[1024,768]{1,0:T(8,128)(2,1)}, u32[]{:S(2)}, u32[]{:S(2)}) collective-permute-start(bf16[1024,768]{1,0:T(8,128)(2,1)} %get-tuple-element.125), channel_id=1, source_target_pairs={{0,1},{1,0},{2,3},{3,2},{4,5},{5,4},{6,7},{7,6},{8,9},{9,8},{10,11... | collective-permute-start | bytes 4718600 | tf_op jit(solution)/shard_map/ppermute | solution.py:35
  330.2 29.7 %all-to-all-start.2 = ((bf16[16,32,768]{2,1,0:T(8,128)(2,1)}), bf16[16,32,768]{2,1,0:T(8,128)(2,1)S(1)}, u32[]{:S(2)}, u32[]{:S(2)}) async-start(bf16[16,32,768]{2,1,0:T(8,128)(2,1)} %get-tuple-element.120), calls=%async_computation.2 | async-start | bytes 1572864 | tf_op jit(solution)/shard_map/all_to_all | solution.py:275
  375.4 27.6 %collective-permute-start.36 = (bf16[4,2,48,1536]{3,2,0,1:T(8,128)(2,1)}, bf16[4,2,48,1536]{3,2,0,1:T(8,128)(2,1)}, u32[]{:S(2)}, u32[]{:S(2)}) collective-permute-start(bf16[4,2,48,1536]{3,2,0,1:T(8,128)(2,1)} %bitcast.163), channel_id=1, source_target_pairs={{0,2},{2,0},{4,6},{6,4},{8,10},{10,8},{12,14},{14,12},{16,18},{18,... | collective-permute-start | bytes 3538952 | tf_op jit(solution)/shard_map/ppermute | solution.py:35
  386.4 36.6 %collective-permute-start.31 = (bf16[4,2,48,1536]{3,2,0,1:T(8,128)(2,1)}, bf16[4,2,48,1536]{3,2,0,1:T(8,128)(2,1)}, u32[]{:S(2)}, u32[]{:S(2)}) collective-permute-start(bf16[4,2,48,1536]{3,2,0,1:T(8,128)(2,1)} %bitcast.164), channel_id=1, source_target_pairs={{0,4},{2,6},{4,0},{6,2},{8,12},{10,14},{12,8},{14,10},{16,20},{18,... | collective-permute-start | bytes 3538952 | tf_op jit(solution)/shard_map/ppermute | solution.py:35
  392.4 37.8 %collective-permute-start.19 = (bf16[1024,768]{1,0:T(8,128)(2,1)}, bf16[1024,768]{1,0:T(8,128)(2,1)S(1)}, u32[]{:S(2)}, u32[]{:S(2)}) collective-permute-start(bf16[1024,768]{1,0:T(8,128)(2,1)} %get-tuple-element.127), channel_id=1, source_target_pairs={{0,1},{1,0},{2,3},{3,2},{4,5},{5,4},{6,7},{7,6},{8,9},{9,8},{10,11... | collective-permute-start | bytes 4718600 | tf_op jit(solution)/shard_map/ppermute | solution.py:35
  393.4 34.3 %all-to-all-start.1 = ((bf16[16,32,768]{2,1,0:T(8,128)(2,1)}), bf16[16,32,768]{2,1,0:T(8,128)(2,1)}, u32[]{:S(2)}, u32[]{:S(2)}) async-start(bf16[16,32,768]{2,1,0:T(8,128)(2,1)} %bitcast.185), calls=%async_computation.1 | async-start | bytes 1572864 | tf_op jit(solution)/shard_map/all_to_all | solution.py:281
  405.9 93.1 %collective-permute-start.37 = (bf16[4,48,1536]{2,1,0:T(8,128)(2,1)}, bf16[4,48,1536]{2,1,0:T(8,128)(2,1)}, u32[]{:S(2)}, u32[]{:S(2)}) collective-permute-start(bf16[4,48,1536]{2,1,0:T(8,128)(2,1)} %dynamic-slice_bitcast_fusion), channel_id=1, source_target_pairs={{0,4},{2,6},{4,0},{6,2},{8,12},{10,14},{12,8},{14,10},{16,20},{18,... | collective-permute-start | bytes 1769480 | tf_op jit(solution)/shard_map/ppermute | solution.py:35
  426.5 77.2 %collective-permute-start.32 = (bf16[4,48,1536]{2,1,0:T(8,128)(2,1)}, bf16[4,48,1536]{2,1,0:T(8,128)(2,1)}, u32[]{:S(2)}, u32[]{:S(2)}) collective-permute-start(bf16[4,48,1536]{2,1,0:T(8,128)(2,1)} %dynamic-slice_bitcast_fusion.1), channel_id=1, source_target_pairs={{0,2},{2,0},{4,6},{6,4},{8,10},{10,8},{12,14},{14,12},{16,18},{18,... | collective-permute-start | bytes 1769480 | tf_op jit(solution)/shard_map/ppermute | solution.py:35
  494.6 31.4 %collective-permute-start.21 = (bf16[4,2,48,768]{3,2,0,1:T(8,128)(2,1)}, bf16[4,2,48,768]{3,2,0,1:T(8,128)(2,1)}, u32[]{:S(2)}, u32[]{:S(2)}) collective-permute-start(bf16[4,2,48,768]{3,2,0,1:T(8,128)(2,1)} %bitcast.168), channel_id=1, source_target_pairs={{0,2},{2,0},{4,6},{6,4},{8,10},{10,8},{12,14},{14,12},{16,18},{18,... | collective-permute-start | bytes 1769480 | tf_op jit(solution)/shard_map/ppermute | solution.py:35
  495.5 32.6 %collective-permute-start.26 = (bf16[4,2,48,768]{3,2,0,1:T(8,128)(2,1)}, bf16[4,2,48,768]{3,2,0,1:T(8,128)(2,1)}, u32[]{:S(2)}, u32[]{:S(2)}) collective-permute-start(bf16[4,2,48,768]{3,2,0,1:T(8,128)(2,1)} %bitcast.167), channel_id=1, source_target_pairs={{0,4},{2,6},{4,0},{6,2},{8,12},{10,14},{12,8},{14,10},{16,20},{18,... | collective-permute-start | bytes 1769480 | tf_op jit(solution)/shard_map/ppermute | solution.py:35
  531.9 36.2 %all-to-all-start.3 = ((bf16[16,32,768]{2,1,0:T(8,128)(2,1)}), bf16[16,32,768]{2,1,0:T(8,128)(2,1)S(1)}, u32[]{:S(2)}, u32[]{:S(2)}) async-start(bf16[16,32,768]{2,1,0:T(8,128)(2,1)} %bitcast.23), calls=%async_computation.3 | async-start | bytes 1572864 | tf_op jit(solution)/shard_map/all_to_all | solution.py:281
  539.1 25.2 %collective-permute-start.24 = (bf16[48,768]{1,0:T(8,128)(2,1)S(1)}, bf16[48,768]{1,0:T(8,128)(2,1)S(1)}, u32[]{:S(2)}, u32[]{:S(2)}) collective-permute-start(bf16[48,768]{1,0:T(8,128)(2,1)S(1)} %get-tuple-element.83), channel_id=1, source_target_pairs={{0,16},{2,18},{4,20},{6,22},{8,24},{10,26},{12,28},{14,30},{16,0},... | collective-permute-start | bytes 221192 | tf_op jit(solution)/shard_map/ppermute | solution.py:35
  (78 other events, 892.7 us)
Sparse Core Ops, SparseCore 0:
  33.5 76.7 all-gather.1
